TPU v7x, 256 devices: a whole 4x4x8 slice. The times are simulated.
256 devices in a mesh: stn: 2 (over core), tm: 32 (over x, z_hi, y), ct: 4 (over z_lo).
Axes of the slice: x: 4, y: 4, z: 8 (z_hi: 2, z_lo: 4; z = z_hi * 4 + z_lo), core: 2. Of those that a mesh axis runs over, the one named last changes fastest.
Arguments:
- voltages: bfloat16 [2, 64, 2097152], P(None, ('stn', 'ct'), 'tm'), may hold values from -128 to 127, as said below
- delays: int32 [64], P(('stn', 'ct')), may hold values from 0 to 4095
Outputs:
- visibilities: float32 [2, 4096, 64, 64], P(None, ('tm', 'ct'), 'stn')
Inputs may be any that keep to these rules, and one draw needn't show every extreme that they name: `voltages`: every entry is a whole number.
All inputs are finite; a program needn't handle non-finite values.
Results may differ from a plain program's by a relative error of at most 0.0037.
Values may be sent and summed in bfloat16 or wider, within the bound.
A program may use at most 128 MiB of HBM per device.

v0:
```python
import math
import jax
import jax.numpy as jnp
from jax import lax
from jax.sharding import PartitionSpec as P

CHANNELS = 4096
RADIX = 64
TAPS = 16


def passed_along(block, axis, distance):
    devices = range(lax.axis_size(axis))
    route = [(i - distance, i) for i in devices if i - distance in devices]
    return lax.ppermute(block, axis, route)


def filter_table():
    length = TAPS * CHANNELS
    index = jnp.arange(length, dtype=jnp.int32).astype(jnp.float32)
    centred = (index - length / 2) / CHANNELS
    window = 0.5 - 0.5 * jnp.cos(2.0 * math.pi * index / length)
    factor = 1.0 / (48.0 * math.sqrt(CHANNELS))
    return (jnp.sinc(centred) * window * factor).reshape(TAPS, CHANNELS)


def dft_block(radix):
    steps = jnp.arange(radix, dtype=jnp.int32)
    grid = steps[:, None] * steps[None, :] % radix
    angle = 2.0 * math.pi * grid.astype(jnp.float32) / radix
    cosine = jnp.cos(angle)
    sine = jnp.sin(angle)
    upper = jnp.concatenate([cosine, sine], axis=1)
    lower = jnp.concatenate([-sine, cosine], axis=1)
    return jnp.concatenate([upper, lower], axis=0).astype(jnp.bfloat16)


def twiddles():
    second = CHANNELS // RADIX
    rows = jnp.arange(second, dtype=jnp.int32)
    cols = jnp.arange(RADIX, dtype=jnp.int32)
    grid = rows[:, None] * cols[None, :] % CHANNELS
    angle = 2.0 * math.pi * grid.astype(jnp.float32) / CHANNELS
    return (jnp.cos(angle), jnp.sin(angle))


def filtered(framed, table):
    count = framed.shape[-2] - TAPS + 1
    total = jnp.zeros(framed.shape[:-2] + (count, CHANNELS), jnp.float32)
    for tap in range(TAPS):
        begin = TAPS - 1 - tap
        total = total + table[tap] * framed[..., begin : begin + count, :].astype(jnp.float32)
    return total.astype(jnp.bfloat16)


def transform(branches):
    second = CHANNELS // RADIX
    number = branches.shape[0]
    stacked = branches.reshape(number, 2 * second, RADIX)
    inner = jnp.einsum(
        "kj,nja->nka", dft_block(second), stacked, preferred_element_type=jnp.float32
    )
    inner = inner.reshape(number, 2, second, RADIX)
    tw_cos, tw_sin = twiddles()
    real_part = inner[:, 0] * tw_cos + inner[:, 1] * tw_sin
    imag_part = inner[:, 1] * tw_cos - inner[:, 0] * tw_sin
    turned = (
        jnp.stack([real_part, imag_part], axis=2)
        .reshape(number, second, 2 * RADIX)
        .astype(jnp.bfloat16)
    )
    result = jnp.einsum("lj,nkj->nlk", dft_block(RADIX), turned, preferred_element_type=jnp.float32)
    return result.reshape(number, 2, CHANNELS).astype(jnp.bfloat16)


def pick_span(row, offset, span):
    return lax.dynamic_slice_in_dim(row, CHANNELS - offset, span, 1)


def on_device(voltages, delays):
    in_count = voltages.shape[1]
    frame_count = voltages.shape[2] // CHANNELS
    prior = passed_along(voltages, "tm", 1)
    extended = jnp.concatenate([prior, voltages], axis=2)
    span = (frame_count + TAPS - 1) * CHANNELS
    shifted = jax.vmap(
        lambda row, offset: pick_span(row, offset, span), in_axes=(1, 0), out_axes=1
    )(extended, delays)
    framed = shifted.reshape(2, in_count, frame_count + TAPS - 1, CHANNELS)
    branches = jnp.moveaxis(filtered(framed, filter_table()), 0, 2)
    spectra = transform(branches.reshape(in_count * frame_count, 2, CHANNELS))
    spectra = spectra.reshape(in_count, frame_count, 2, CHANNELS)
    moved = lax.all_to_all(
        lax.all_to_all(spectra, "tm", split_axis=3, concat_axis=1, tiled=True),
        "ct",
        split_axis=3,
        concat_axis=0,
        tiled=True,
    )
    local = moved.transpose(3, 2, 0, 1)
    total_frames = local.shape[3]
    swapped = jnp.stack([local[:, 1], -local[:, 0]], axis=1)
    left = jnp.stack([local, swapped], axis=0)
    summed = jnp.einsum(
        "ocjaf,cjbf->ocab",
        left,
        lax.all_gather(local, "stn", axis=2, tiled=True),
        preferred_element_type=jnp.float32,
    )
    return summed * (1.0 / total_frames)


def solution(mesh):
    return jax.shard_map(
        on_device,
        mesh=mesh,
        in_specs=(P(None, ("stn", "ct"), "tm"), P(("stn", "ct"))),
        out_specs=P(None, ("tm", "ct"), "stn", None),
        check_vma=False,
    )
```

profile of v0, /device:TPU:1, one launch (start us, length us, event | category | flops | bytes accessed | tf_op | source)
XLA Modules:
  0.0 411.2 jit_solution(17613483547774946661)
XLA Ops:
  6.5 3.8 copy.57
  10.3 5.4 %collective-permute-start = (bf16[2,8,65536]{2,0,1:T(2,128)(2,1)S(1)}, bf16[2,8,65536]{2,0,1:T(2,128)(2,1)}, u32[]{:S(2)}, u32[]{:S(2)}) collective-permute-start(bf16[2,8,65536]{2,0,1:T(2,128)(2,1)S(1)} %copy.57), channel_id=1, source_target_pairs={{0,4},{4,8},{8,12},{12,16},{16,20},{20,24},{24,28},{28,32},{32,36}... | collective-permute-start | bytes 6291464 | tf_op jit(solution)/shard_map/ppermute | solution.py:15
  17.4 41.2 %collective-permute-done = bf16[2,8,65536]{2,0,1:T(2,128)(2,1)} collective-permute-done((bf16[2,8,65536]{2,0,1:T(2,128)(2,1)S(1)}, bf16[2,8,65536]{2,0,1:T(2,128)(2,1)}, u32[]{:S(2)}, u32[]{:S(2)}) %collective-permute-start) | collective-permute-done | bytes 2097184 | tf_op jit(solution)/shard_map/ppermute | solution.py:15
  58.6 7.1 %maximum_bitcast_fusion = bf16[8,2,131072]{2,1,0:T(2,128)(2,1)} fusion(bf16[2,8,65536]{2,0,1:T(2,128)(2,1)S(1)} %copy.57, bf16[2,8,65536]{2,0,1:T(2,128)(2,1)} %collective-permute-done), kind=kLoop, calls=%fused_computation.2 | loop fusion | flops 8388608 | bytes 8388608 | tf_op jit(solution)/shard_map/vmap()/transpose | solution.py:77
  65.8 34.8 %while.1 = (s32[]{:T(128)}, bf16[8,2,131072]{2,1,0:T(2,128)(2,1)}, s32[8,3]{0,1:T(4,128)S(1)}, bf16[8,2,126976]{2,1,0:T(2,128)(2,1)}, s32[]{:T(128)}) while((s32[]{:T(128)}, bf16[8,2,131072]{2,1,0:T(2,128)(2,1)}, s32[8,3]{0,1:T(4,128)S(1)}, bf16[8,2,126976]{2,1,0:T(2,128)(2,1)}, s32[]{:T(128)}) %tuple.41), condition=%wide.while_cond, body=%wide.while_body.sunk | while | flops 2 | bytes 1016949 | solution.py:77
  66.4 3.7 dynamic-slice_dynamic-update-slice_fusion.2
  70.7 3.7 dynamic-slice_dynamic-update-slice_fusion.2
  75.1 3.7 dynamic-slice_dynamic-update-slice_fusion.2
  79.5 3.7 dynamic-slice_dynamic-update-slice_fusion.2
  83.8 3.7 dynamic-slice_dynamic-update-slice_fusion.2
  88.2 3.7 dynamic-slice_dynamic-update-slice_fusion.2
  92.5 3.7 dynamic-slice_dynamic-update-slice_fusion.2
  96.8 3.7 dynamic-slice_dynamic-update-slice_fusion.2
  100.6 4.4 %copy.59 = bf16[8,2,126976]{2,0,1:T(8,128)(2,1)S(1)} copy(bf16[8,2,126976]{2,1,0:T(2,128)(2,1)} %get-tuple-element.12) | data formatting | bytes 8126464 | tf_op jit(solution)/shard_map/vmap()/gather | solution.py:77
  105.0 8.8 %fusion.5 = bf16[8,16,2,4096]{3,0,1,2:T(8,128)(2,1)S(1)} fusion(bf16[2,8,31,4096]{3,1,2,0:T(8,128)(2,1)S(1)} %bitcast.81, f32[4096]{0:T(1024)S(1)} %get-tuple-element.32, f32[4096]{0:T(1024)S(1)} %get-tuple-element.33, f32[4096]{0:T(1024)S(1)} %get-tuple-element.34, f32[4096]{0:T(1024)S(1)} %get-tuple-element.35, f32[4096]{0:T(1024)S(1)} %get-tuple-element.36, ...), kind=kLoop, calls=%fused_computation.16 | loop fusion | flops 50331648 | bytes 35913728 | tf_op jit(solution)/shard_map/transpose | solution.py:90
  113.8 2.2 copy.60
  116.0 4.2 %reshape_reshape.3 = bf16[128,128,64]{2,1,0:T(8,128)(2,1)} reshape(bf16[8,16,2,4096]{3,2,1,0:T(2,128)(2,1)S(1)} %copy.60) | data formatting | bytes 4194304 | tf_op jit(solution)/shard_map/reshape;reshape | solution.py:59
  120.1 4.8 %copy.61 = bf16[128,128,64]{1,0,2:T(8,128)(2,1)S(1)} copy(bf16[128,128,64]{2,1,0:T(8,128)(2,1)} %reshape_reshape.3) | data formatting | bytes 4194304 | tf_op jit(solution)/shard_map/reshape;reshape | solution.py:59
  126.3 5.0 %add_convert_fusion.1 = (bf16[128,64,1,64]{0,3,2,1:T(8,128)(2,1)S(1)}, bf16[128,64,1,64]{0,3,2,1:T(8,128)(2,1)S(1)}) fusion(f32[128,1,64,64]{0,2,1,3:T(8,128)S(1)} %get-tuple-element.26, f32[128,1,64,64]{0,2,1,3:T(8,128)S(1)} %get-tuple-element.25, f32[64,64]{1,0:T(8,128)S(1)} %get-tuple-element.49, f32[64,64]{1,0:T(8,128)S(1)} %get-tuple-element.50), kind=kLoop, calls=%fused_computation.15 | loop fusion | flops 4194304 | bytes 6324224 | tf_op jit(solution)/shard_map/convert
  132.3 3.9 copy.65
  136.2 6.7 %convert_element_type.154 = bf16[8,16,2,4096]{3,2,1,0:T(2,128)(2,1)S(1)} reshape(bf16[128,128,64]{2,1,0:T(8,128)(2,1)} %copy.65) | data formatting | bytes 4194304 | tf_op jit(solution)/shard_map/convert_element_type | solution.py:73
  142.9 16.7 %copy.66 = bf16[8,16,2,4096]{1,0,2,3:T(8,128)(2,1)} copy(bf16[8,16,2,4096]{3,2,1,0:T(2,128)(2,1)S(1)} %convert_element_type.154) | data formatting | bytes 4194304 | tf_op jit(solution)/shard_map/convert_element_type | solution.py:73
  159.6 19.7 %reshape.171 = bf16[32,2,16384]{2,1,0:T(2,128)(2,1)S(1)} reshape(bf16[4096,2,8,16]{3,2,1,0:T(8,128)(2,1)} %bitcast.82) | data formatting | bytes 4194304
  179.4 59.7 %all_to_all.36 = bf16[32,2,16384]{2,1,0:T(2,128)(2,1)} all-to-all(bf16[32,2,16384]{2,1,0:T(2,128)(2,1)S(1)} %reshape.171), channel_id=1, replica_groups=mesh['stn'=2,'tm'=32,'ct'=4] {'tm'}, dimensions={0} | all-to-all | bytes 4194304 | tf_op jit(solution)/shard_map/all_to_all | solution.py:94
  239.1 16.5 %reshape.172 = bf16[4096,2,8,16]{3,2,1,0:T(8,128)(2,1)} reshape(bf16[32,2,16384]{2,1,0:T(2,128)(2,1)} %all_to_all.36) | data formatting | bytes 4194304
  255.5 15.3 %copy.68 = bf16[8,32,16,2,128]{4,2,1,3,0:T(8,128)(2,1)S(1)} copy(bf16[8,32,16,2,128]{2,0,3,4,1:T(8,128)(2,1)} %bitcast.83) | data formatting | bytes 4194304 | tf_op jit(solution)/shard_map/all_to_all | solution.py:94
  270.8 4.0 copy.69
  274.8 104.3 %all_to_all.37 = bf16[8,512,2,128]{1,2,0,3:T(2,128)(2,1)S(1)} all-to-all(bf16[8,512,2,128]{1,2,0,3:T(2,128)(2,1)} %copy.69), channel_id=1, replica_groups=mesh['stn'=2,'tm'=32,'ct'=4] {'ct'}, dimensions={3} | all-to-all | bytes 4194304 | tf_op jit(solution)/shard_map/all_to_all | solution.py:93
  380.2 2.5 copy.93
  382.8 1.8 fusion.57
  386.2 13.0 %all-gather.2.cloned.1.call-done = bf16[32,2,64,512]{3,2,1,0:T(8,128)(2,1)} async-done(((bf16[32,2,32,512]{3,2,1,0:T(8,128)(2,1)}), bf16[32,2,64,512]{3,2,1,0:T(8,128)(2,1)}) %all-gather.2.cloned.1.call-update) | async-done | bytes 4194320 | tf_op jit(solution)/shard_map/all_gather | solution.py:107
  399.1 4.1 fusion.16
  (38 shorter events, 13.0 us)
Async XLA Ops:
  6.5 9.2 %copy-start.1 = (s32[8]{0:T(128)S(1)}, s32[8]{0:T(128)}, u32[]{:S(2)}) copy-start(s32[8]{0:T(128)} %param.3) | copy-start | bytes 100
  6.5 392.6 %all-gather.2.cloned.1.call-start = ((), (), s32[]{:S(2)}) async-start(), calls=%async_computation.2 | async-start | bytes 6291456 | tf_op jit(solution)/shard_map/all_gather | solution.py:107
  10.3 48.3 %collective-permute-start = (bf16[2,8,65536]{2,0,1:T(2,128)(2,1)S(1)}, bf16[2,8,65536]{2,0,1:T(2,128)(2,1)}, u32[]{:S(2)}, u32[]{:S(2)}) collective-permute-start(bf16[2,8,65536]{2,0,1:T(2,128)(2,1)S(1)} %copy.57), channel_id=1, source_target_pairs={{0,4},{4,8},{8,12},{12,16},{16,20},{20,24},{24,28},{28,32},{32,36}... | collective-permute-start | bytes 6291464 | tf_op jit(solution)/shard_map/ppermute | solution.py:15
  382.8 16.4 %copy-start = (bf16[4,8,512,2,32]{2,1,0,3,4:T(8,128)(2,1)S(1)}, bf16[4,8,512,2,32]{2,1,0,3,4:T(8,128)(2,1)}, u32[]{:S(2)}) copy-start(bf16[4,8,512,2,32]{2,1,0,3,4:T(8,128)(2,1)} %copy.93) | copy-start | bytes 6291460
Sparse Core Ops, SparseCore 0:
  382.9 16.2 all-gather.1
where the time goes:
time: 413 us; the launch traced here: 411 us
  blocking collectives  164 us (40%)
  local copies, waits for them, and re-layouts  142 us (34%)
  waiting for transfers between devices  54.2 us (13%)
  other arithmetic  26.1 us (6%)
  between operations  13.5 us (3%)
  matrix products  5.65 us (1%)
  starting transfers between devices  5.4 us (1%)
    all_to_all x1, blocking collectives, on_device(): lax.all_to_all(lax.all_to_all(spectra, 'tm', split_axis=3, concat_axis=1,...  104 us
    all_to_all x1, blocking collectives, on_device(): lax.all_to_all(spectra, 'tm', split_axis=3, concat_axis=1, tiled=True)  59.7 us
    ppermute x1, waiting for transfers between devices, passed_along(): return lax.ppermute(block, axis, route)  41.2 us
    unnamed x8, local copies, waits for them, and re-layouts  39.9 us
    gather x24, local copies, waits for them, and re-layouts  34.8 us
    convert_element_type x3, local copies, waits for them, and re-layouts, transform(): return result.reshape(number, 2, CHANNELS).astype(jnp.bfloat16)  27.4 us
    all_to_all x2, local copies, waits for them, and re-layouts, on_device(): lax.all_to_all(spectra, 'tm', split_axis=3, concat_axis=1, tiled=True)  19.3 us
    all_gather x1, waiting for transfers between devices, on_device(): lax.all_gather(local, 'stn', axis=2, tiled=True)  13 us
  transfers between devices with their start and end apart: 2, of which 2 were waited for; matrix products, arithmetic and copies ran while one was open for 1% of the time, Pallas kernels for 0%

commit v1 on v0

--- a/solution.py
+++ b/solution.py
@@ -90,12 +90,10 @@
     branches = jnp.moveaxis(filtered(framed, filter_table()), 0, 2)
     spectra = transform(branches.reshape(in_count * frame_count, 2, CHANNELS))
     spectra = spectra.reshape(in_count, frame_count, 2, CHANNELS)
-    moved = lax.all_to_all(
-        lax.all_to_all(spectra, "tm", split_axis=3, concat_axis=1, tiled=True),
-        "ct",
-        split_axis=3,
-        concat_axis=0,
-        tiled=True,
+    inputs = lax.all_to_all(spectra, "tm", split_axis=3, concat_axis=1, tiled=True)
+    moved = jnp.concatenate(
+        jax.lax.all_to_all(jnp.stack(jnp.split(inputs, jax.lax.psum(1, "ct"), 3)), "ct", 0, 0),
+        axis=0,
     )
     local = moved.transpose(3, 2, 0, 1)
     total_frames = local.shape[3]

time: 413 us -> 423 us (1.024)
  local copies, waits for them, and re-layouts: 142 us -> 156 us
    another operation x0 -> x6, local copies, waits for them, and re-layouts: none -> 16.6 us  [the longest x5 12.3 us: on_device(): jnp.stack(jnp.split(inputs, jax.lax.psum(1, 'ct'), 3))]
    all_to_all x2 -> x1, local copies, waits for them, and re-layouts: 19.3 us -> 15.3 us  [on_device(): lax.all_to_all(spectra, 'tm', split_axis=3, concat_axis=1, tiled=True)]
    unnamed x8 -> x14, local copies, waits for them, and re-layouts: 39.9 us -> 41.3 us
  transfers between devices with their start and end apart: 2 -> 2, of which waited for: 2 -> 2; matrix products, arithmetic and copies ran while one was open for 1% -> 2% of each run, Pallas kernels for 0% -> 0%
where the time goes in v1:
time: 423 us; the launch traced here: 421 us
  blocking collectives  164 us (39%)
  local copies, waits for them, and re-layouts  156 us (37%)
  waiting for transfers between devices  51.6 us (12%)
  other arithmetic  25.9 us (6%)
  between operations  13.6 us (3%)
  matrix products  5.65 us (1%)
  starting transfers between devices  5.4 us (1%)
    all_to_all x1, blocking collectives, on_device(): jax.lax.all_to_all(jnp.stack(jnp.split(inputs, jax.lax.psum(1, 'ct'), 3))...  104 us
    all_to_all x1, blocking collectives, on_device(): lax.all_to_all(spectra, 'tm', split_axis=3, concat_axis=1, tiled=True)  59.7 us
    unnamed x14, local copies, waits for them, and re-layouts  41.3 us
    ppermute x1, waiting for transfers between devices, passed_along(): return lax.ppermute(block, axis, route)  41.2 us
    gather x24, local copies, waits for them, and re-layouts  35.3 us
    convert_element_type x3, local copies, waits for them, and re-layouts, transform(): return result.reshape(number, 2, CHANNELS).astype(jnp.bfloat16)  27.4 us
    all_to_all x1, local copies, waits for them, and re-layouts, on_device(): lax.all_to_all(spectra, 'tm', split_axis=3, concat_axis=1, tiled=True)  15.3 us
    another operation x5, local copies, waits for them, and re-layouts, on_device(): jnp.stack(jnp.split(inputs, jax.lax.psum(1, 'ct'), 3))  12.3 us
  transfers between devices with their start and end apart: 2, of which 2 were waited for; matrix products, arithmetic and copies ran while one was open for 2% of the time, Pallas kernels for 0%

profile of v1, /device:TPU:1, one launch (start us, length us, event | category | flops | bytes accessed | tf_op | source)
XLA Modules:
  0.0 421.4 jit_solution(15673680900924384325)
XLA Ops:
  6.5 3.8 copy.47
  10.3 5.4 %collective-permute-start = (bf16[2,8,65536]{2,0,1:T(2,128)(2,1)S(1)}, bf16[2,8,65536]{2,0,1:T(2,128)(2,1)}, u32[]{:S(2)}, u32[]{:S(2)}) collective-permute-start(bf16[2,8,65536]{2,0,1:T(2,128)(2,1)S(1)} %copy.47), channel_id=1, source_target_pairs={{0,4},{4,8},{8,12},{12,16},{16,20},{20,24},{24,28},{28,32},{32,36}... | collective-permute-start | bytes 6291464 | tf_op jit(solution)/shard_map/ppermute | solution.py:15
  17.4 41.2 %collective-permute-done = bf16[2,8,65536]{2,0,1:T(2,128)(2,1)} collective-permute-done((bf16[2,8,65536]{2,0,1:T(2,128)(2,1)S(1)}, bf16[2,8,65536]{2,0,1:T(2,128)(2,1)}, u32[]{:S(2)}, u32[]{:S(2)}) %collective-permute-start) | collective-permute-done | bytes 2097184 | tf_op jit(solution)/shard_map/ppermute | solution.py:15
  58.6 7.1 %maximum_bitcast_fusion = bf16[8,2,131072]{2,1,0:T(2,128)(2,1)} fusion(bf16[2,8,65536]{2,0,1:T(2,128)(2,1)S(1)} %copy.47, bf16[2,8,65536]{2,0,1:T(2,128)(2,1)} %collective-permute-done), kind=kLoop, calls=%fused_computation.2 | loop fusion | flops 8388608 | bytes 8388608 | tf_op jit(solution)/shard_map/vmap()/transpose | solution.py:77
  65.8 35.3 %while.1 = (s32[]{:T(128)}, bf16[8,2,131072]{2,1,0:T(2,128)(2,1)}, s32[8,3]{0,1:T(4,128)S(1)}, bf16[8,2,126976]{2,1,0:T(2,128)(2,1)}, s32[]{:T(128)}) while((s32[]{:T(128)}, bf16[8,2,131072]{2,1,0:T(2,128)(2,1)}, s32[8,3]{0,1:T(4,128)S(1)}, bf16[8,2,126976]{2,1,0:T(2,128)(2,1)}, s32[]{:T(128)}) %tuple.42), condition=%wide.while_cond, body=%wide.while_body.sunk | while | flops 2 | bytes 1016949 | solution.py:77
  66.4 3.7 dynamic-slice_dynamic-update-slice_fusion.2
  70.8 3.7 dynamic-slice_dynamic-update-slice_fusion.2
  75.2 3.8 dynamic-slice_dynamic-update-slice_fusion.2
  79.7 3.7 dynamic-slice_dynamic-update-slice_fusion.2
  84.1 3.7 dynamic-slice_dynamic-update-slice_fusion.2
  88.5 3.7 dynamic-slice_dynamic-update-slice_fusion.2
  92.9 3.7 dynamic-slice_dynamic-update-slice_fusion.2
  97.3 3.8 dynamic-slice_dynamic-update-slice_fusion.2
  101.1 4.4 %copy.49 = bf16[8,2,126976]{2,0,1:T(8,128)(2,1)S(1)} copy(bf16[8,2,126976]{2,1,0:T(2,128)(2,1)} %get-tuple-element.12) | data formatting | bytes 8126464 | tf_op jit(solution)/shard_map/vmap()/gather | solution.py:77
  105.5 8.8 %fusion.5 = bf16[8,16,2,4096]{3,0,1,2:T(8,128)(2,1)S(1)} fusion(bf16[2,8,31,4096]{3,1,2,0:T(8,128)(2,1)S(1)} %bitcast.83, f32[4096]{0:T(1024)S(1)} %get-tuple-element.34, f32[4096]{0:T(1024)S(1)} %get-tuple-element.35, f32[4096]{0:T(1024)S(1)} %get-tuple-element.36, f32[4096]{0:T(1024)S(1)} %get-tuple-element.37, f32[4096]{0:T(1024)S(1)} %get-tuple-element.38, ...), kind=kLoop, calls=%fused_computation.22 | loop fusion | flops 50331648 | bytes 35913728 | tf_op jit(solution)/shard_map/transpose | solution.py:90
  116.5 4.2 reshape_reshape.3
  120.6 4.8 %copy.51 = bf16[128,128,64]{1,0,2:T(8,128)(2,1)S(1)} copy(bf16[128,128,64]{2,1,0:T(8,128)(2,1)} %reshape_reshape.3) | data formatting | bytes 4194304 | tf_op jit(solution)/shard_map/reshape;reshape | solution.py:59
  126.8 5.0 %add_convert_fusion.1 = (bf16[128,64,1,64]{0,3,2,1:T(8,128)(2,1)S(1)}, bf16[128,64,1,64]{0,3,2,1:T(8,128)(2,1)S(1)}) fusion(f32[128,1,64,64]{0,2,1,3:T(8,128)S(1)} %get-tuple-element.26, f32[128,1,64,64]{0,2,1,3:T(8,128)S(1)} %get-tuple-element.25, f32[64,64]{1,0:T(8,128)S(1)} %get-tuple-element.51, f32[64,64]{1,0:T(8,128)S(1)} %get-tuple-element.52), kind=kLoop, calls=%fused_computation.21 | loop fusion | flops 4194304 | bytes 6324224 | tf_op jit(solution)/shard_map/convert
  132.8 3.9 copy.55
  136.7 6.7 %convert_element_type.154 = bf16[8,16,2,4096]{3,2,1,0:T(2,128)(2,1)S(1)} reshape(bf16[128,128,64]{2,1,0:T(8,128)(2,1)} %copy.55) | data formatting | bytes 4194304 | tf_op jit(solution)/shard_map/convert_element_type | solution.py:73
  143.5 16.7 %copy.56 = bf16[8,16,2,4096]{1,0,2,3:T(8,128)(2,1)} copy(bf16[8,16,2,4096]{3,2,1,0:T(2,128)(2,1)S(1)} %convert_element_type.154) | data formatting | bytes 4194304 | tf_op jit(solution)/shard_map/convert_element_type | solution.py:73
  160.2 19.7 %reshape.175 = bf16[32,2,16384]{2,1,0:T(2,128)(2,1)S(1)} reshape(bf16[4096,2,8,16]{3,2,1,0:T(8,128)(2,1)} %bitcast.84) | data formatting | bytes 4194304
  179.9 59.7 %all_to_all.23 = bf16[32,2,16384]{2,1,0:T(2,128)(2,1)} all-to-all(bf16[32,2,16384]{2,1,0:T(2,128)(2,1)S(1)} %reshape.175), channel_id=1, replica_groups=mesh['stn'=2,'tm'=32,'ct'=4] {'tm'}, dimensions={0} | all-to-all | bytes 4194304 | tf_op jit(solution)/shard_map/all_to_all | solution.py:93
  239.6 16.5 %reshape.176 = bf16[4096,2,8,16]{3,2,1,0:T(8,128)(2,1)} reshape(bf16[32,2,16384]{2,1,0:T(2,128)(2,1)} %all_to_all.23) | data formatting | bytes 4194304
  256.1 15.3 %copy.58 = bf16[8,32,16,2,128]{4,2,1,3,0:T(8,128)(2,1)S(1)} copy(bf16[8,32,16,2,128]{2,0,3,4,1:T(8,128)(2,1)} %bitcast.85) | data formatting | bytes 4194304 | tf_op jit(solution)/shard_map/all_to_all | solution.py:93
  271.4 4.4 %slice_bitcast_fusion.3 = (bf16[1,8,512,2,32]{4,2,3,1,0:T(8,128)(2,1)}, bf16[1,8,512,2,32]{4,2,3,1,0:T(8,128)(2,1)}, bf16[1,8,512,2,32]{4,2,3,1,0:T(8,128)(2,1)}, bf16[1,8,512,2,32]{4,2,3,1,0:T(8,128)(2,1)}) fusion(bf16[8,512,2,128]{3,1,2,0:T(8,128)(2,1)S(1)} %bitcast.86), kind=kLoop, calls=%fused_computation.12 | loop fusion | bytes 4194304 | tf_op jit(solution)/shard_map/stack | solution.py:95
  279.6 2.6 copy.61
  285.1 104.1 %all_to_all.24 = bf16[4,8,512,2,32]{2,4,3,1,0:T(8,128)(2,1)S(1)} all-to-all(bf16[4,8,512,2,32]{2,4,3,1,0:T(8,128)(2,1)S(1)} %pad_maximum_fusion.1), channel_id=1, replica_groups=mesh['stn'=2,'tm'=32,'ct'=4] {'ct'}, dimensions={0} | all-to-all | bytes 4194304 | tf_op jit(solution)/shard_map/all_to_all | solution.py:95
  390.6 2.5 copy.85
  393.1 4.3 %copy.64 = bf16[1,32,2,32,512]{4,3,2,0,1:T(8,128)(2,1)} copy(bf16[1,32,2,32,512]{4,1,2,3,0:T(8,128)(2,1)} %bitcast.89) | data formatting | bytes 4194304 | tf_op jit(solution)/shard_map/stack | solution.py:101
  399.1 10.3 %all-gather.2.cloned.1.call-done = bf16[32,2,64,512]{3,2,1,0:T(8,128)(2,1)} async-done(((bf16[32,2,32,512]{3,2,1,0:T(8,128)(2,1)}), bf16[32,2,64,512]{3,2,1,0:T(8,128)(2,1)}) %all-gather.2.cloned.1.call-update) | async-done | bytes 4194320 | tf_op jit(solution)/shard_map/all_gather | solution.py:105
  409.4 4.1 fusion.16
  (49 shorter events, 22.4 us)
Async XLA Ops:
  6.5 9.2 %copy-start.4 = (s32[8]{0:T(128)S(1)}, s32[8]{0:T(128)}, u32[]{:S(2)}) copy-start(s32[8]{0:T(128)} %param.3) | copy-start | bytes 100
  6.5 402.9 %all-gather.2.cloned.1.call-start = ((), (), s32[]{:S(2)}) async-start(), calls=%async_computation.2 | async-start | bytes 6291456 | tf_op jit(solution)/shard_map/all_gather | solution.py:105
  10.3 48.3 %collective-permute-start = (bf16[2,8,65536]{2,0,1:T(2,128)(2,1)S(1)}, bf16[2,8,65536]{2,0,1:T(2,128)(2,1)}, u32[]{:S(2)}, u32[]{:S(2)}) collective-permute-start(bf16[2,8,65536]{2,0,1:T(2,128)(2,1)S(1)} %copy.47), channel_id=1, source_target_pairs={{0,4},{4,8},{8,12},{12,16},{16,20},{20,24},{24,28},{28,32},{32,36}... | collective-permute-start | bytes 6291464 | tf_op jit(solution)/shard_map/ppermute | solution.py:15
  275.7 6.5 %copy-start.2 = (bf16[1,8,512,2,32]{4,2,3,1,0:T(8,128)(2,1)S(1)}, bf16[1,8,512,2,32]{4,2,3,1,0:T(8,128)(2,1)}, u32[]{:S(2)}) copy-start(bf16[1,8,512,2,32]{4,2,3,1,0:T(8,128)(2,1)} %get-tuple-element.32) | copy-start | bytes 1572868
  389.2 1.4 copy-start.1
  393.1 4.3 %copy-start = (bf16[4,8,512,2,32]{2,1,0,3,4:T(8,128)(2,1)S(1)}, bf16[4,8,512,2,32]{2,1,0,3,4:T(8,128)(2,1)}, u32[]{:S(2)}) copy-start(bf16[4,8,512,2,32]{2,1,0,3,4:T(8,128)(2,1)} %copy.85) | copy-start | bytes 6291460
  397.5 11.9 %copy-start.3 = (bf16[1,32,2,32,512]{4,3,2,0,1:T(8,128)(2,1)S(1)}, bf16[1,32,2,32,512]{4,3,2,0,1:T(8,128)(2,1)}, u32[]{:S(2)}) copy-start(bf16[1,32,2,32,512]{4,3,2,0,1:T(8,128)(2,1)} %copy.64) | copy-start | bytes 6291460
Sparse Core Ops, SparseCore 0:
  393.2 16.1 all-gather.1
